TPU v7x, 32 devices: a whole 2x2x4 slice. The times are simulated.
32 devices in a mesh: ctx: 8 (over z, y), exp: 4 (over x, core).
Axes of the slice: x: 2, y: 2, z: 4, core: 2. Of those that a mesh axis runs over, the one named last changes fastest.
Arguments:
- queries: bfloat16 [1024, 4096], P('ctx', 'exp'), may hold values from -0.5 to 0.5
- attn_keys: bfloat16 [1024, 4096], P('ctx', 'exp'), may hold values from -0.5 to 0.5
- attn_values: bfloat16 [1024, 4096], P('ctx', 'exp'), may hold values from -3 to 3
- out_grad: bfloat16 [1024, 4096], P('ctx', 'exp'), may hold values from -0.75 to 0.75
- log_decay: float32 [1024, 32], P('ctx', 'exp'), may hold values from -1 to 0
- moe_input: bfloat16 [1024, 3072], P(('ctx', 'exp')), may hold values from -6 to 6
- routes: int32 [1024, 2], P(('ctx', 'exp')), may hold values from 0 to 7, all different within a row; in each aligned block of 32 rows (0 to 31, 32 to 63, ...) at most 16 rows name the same one
- route_weight: float32 [1024, 2], P(('ctx', 'exp')), may hold values from 0.25 to 1
- w_gate: bfloat16 [8, 9216, 3072], P('exp', 'ctx'), may hold values from -0.109375 to 0.109375
- w_up: bfloat16 [8, 9216, 3072], P('exp', 'ctx'), may hold values from -0.109375 to 0.109375
- w_down: bfloat16 [8, 9216, 3072], P('exp', 'ctx'), may hold values from -0.0625 to 0.0625
Outputs:
- attn_out: bfloat16 [1024, 4096], P('ctx', 'exp')
- grad_q: bfloat16 [1024, 4096], P('ctx', 'exp')
- grad_k: bfloat16 [1024, 4096], P('ctx', 'exp')
- derivative_wrt_entries: bfloat16 [1024, 4096], P('ctx', 'exp')
- moe_out: bfloat16 [1024, 3072], P(('ctx', 'exp'))
Inputs may be any that keep to these rules, and one draw needn't show every extreme that they name: `routes`: in the rows of one device no expert is named more than 16 times; each row names two different experts.
All inputs are finite; a program needn't handle non-finite values.
Results may differ from a plain program's by a relative error of at most 0.025.
Values may be sent and summed in bfloat16 or wider, within the bound.
No kernel may reach another device: no remote copies, remote signals or barrier semaphores. Data moves between devices by JAX's collectives and lax.ppermute only.
A program may use at most 128 MiB of HBM per device.

v0:
```python
import jax
import jax.numpy as jnp
from jax import lax
from jax.sharding import PartitionSpec as P


def entering(value, axis, combine, identity, reverse):
    length, position = (lax.axis_size(axis), lax.axis_index(axis))
    everything = jax.tree.map(
        lambda part, kind: lax.all_gather(part.astype(kind), axis),
        value,
        (jnp.bfloat16, jnp.bfloat16),
    )
    start = jax.tree.map(
        lambda part, zero: jnp.broadcast_to(jnp.asarray(zero, part.dtype), part.shape),
        value,
        identity,
    )

    def step(k, before):
        at = length - 1 - k if reverse else k
        reached = at > position if reverse else at < position
        new = combine(
            before, jax.tree.map(lambda part, own: part[at].astype(own.dtype), everything, value)
        )
        return jax.tree.map(lambda a, b: jnp.where(reached, a, b), new, before)

    return lax.fori_loop(0, length, step, start)


def chain_combine(earlier, later):
    return (earlier[0] * later[0], later[0][:, None, None] * earlier[1] + later[1])


def attention(queries, attn_keys, attn_values, out_grad, log_decay):
    length = queries.shape[0]
    heads = log_decay.shape[1]
    width = queries.shape[1] // heads
    shaped = (length, heads, width)
    q_heads = queries.reshape(shaped)
    k_heads = attn_keys.reshape(shaped)
    v_heads = attn_values.reshape(shaped)
    gradient_heads = out_grad.reshape(shaped)
    cum_decay = jnp.cumsum(log_decay, axis=0)
    total = cum_decay[length - 1]
    position = jnp.arange(length, dtype=jnp.int32)
    causal = (position[:, None] >= position[None, :])[None]
    spread = cum_decay.T[:, :, None] - cum_decay.T[:, None, :]
    block_weight = jnp.where(causal, jnp.exp(jnp.where(causal, spread, 0.0)), 0.0)
    rising_edge = jnp.exp(cum_decay)[:, :, None]
    falling_edge = jnp.exp(total[None, :] - cum_decay)[:, :, None]
    scaled_queries = q_heads.astype(jnp.float32) * rising_edge
    full_keys = k_heads.astype(jnp.float32)
    full_values = v_heads.astype(jnp.float32)
    scaled_gradient = gradient_heads.astype(jnp.float32) * rising_edge
    running_block_state = jnp.einsum(
        "mly,mlf->lyf", full_keys * falling_edge, full_values, precision=lax.Precision.HIGHEST
    )
    state_gradient = jnp.einsum(
        "nbd,nbw->bdw",
        scaled_queries,
        gradient_heads.astype(jnp.float32),
        precision=lax.Precision.HIGHEST,
    )
    growth = jnp.exp(total)
    identity = (jnp.ones((heads,), jnp.float32), jnp.zeros((heads, width, width), jnp.float32))
    prior_memory_matrix = entering(
        (growth, running_block_state), "ctx", chain_combine, identity, False
    )[1]
    following_state = entering((growth, state_gradient), "ctx", chain_combine, identity, True)[1]
    scores = jnp.einsum("thd,shd->hts", q_heads, k_heads, preferred_element_type=jnp.float32)
    attention_result = (scores * block_weight).astype(jnp.bfloat16)
    layer_output = jnp.einsum(
        "pgm,mpo->gpo", attention_result, v_heads, preferred_element_type=jnp.float32
    )
    layer_output = layer_output + jnp.einsum(
        "bip,ipu->biu", scaled_queries, prior_memory_matrix, precision=lax.Precision.HIGHEST
    )
    dscores = jnp.einsum(
        "thd,shd->hts", gradient_heads, v_heads, preferred_element_type=jnp.float32
    )
    weight_gradient = (dscores * block_weight).astype(jnp.bfloat16)
    query_gradient = jnp.einsum(
        "pgm,mpo->gpo", weight_gradient, k_heads, preferred_element_type=jnp.float32
    )
    query_gradient = query_gradient + jnp.einsum(
        "pig,ijg->pij", scaled_gradient, prior_memory_matrix, precision=lax.Precision.HIGHEST
    )
    key_gradient = jnp.einsum(
        "nkg,knv->gnv", weight_gradient, q_heads, preferred_element_type=jnp.float32
    )
    key_gradient = key_gradient + falling_edge * jnp.einsum(
        "jnr,nbr->jnb", full_values, following_state, precision=lax.Precision.HIGHEST
    )
    value_gradient = jnp.einsum(
        "nkg,knv->gnv", attention_result, gradient_heads, preferred_element_type=jnp.float32
    )
    value_gradient = value_gradient + falling_edge * jnp.einsum(
        "umj,mje->ume", full_keys, following_state, precision=lax.Precision.HIGHEST
    )
    flat_shape = (length, queries.shape[1])
    return (
        layer_output.reshape(flat_shape).astype(jnp.bfloat16),
        query_gradient.reshape(flat_shape).astype(jnp.bfloat16),
        key_gradient.reshape(flat_shape).astype(jnp.bfloat16),
        value_gradient.reshape(flat_shape).astype(jnp.bfloat16),
    )


def route_tables(routes, route_weight, experts, capacity):
    row_count = routes.shape[0]
    flat_routes = routes.reshape(row_count * 2)
    one_hot = (flat_routes[:, None] == jnp.arange(experts, dtype=jnp.int32)[None, :]).astype(
        jnp.int32
    )
    earlier_count = jnp.cumsum(one_hot, axis=0) - one_hot
    slot_index = jnp.sum(earlier_count * one_hot, axis=1)
    target = flat_routes * capacity + slot_index
    member = (jnp.arange(experts * capacity, dtype=jnp.int32)[:, None] == target[None, :]).astype(
        jnp.float32
    )
    picker = member.reshape(experts * capacity, row_count, 2).sum(axis=2)
    merge_lookup = (
        (member * route_weight.reshape(row_count * 2)[None, :])
        .reshape(experts * capacity, row_count, 2)
        .sum(axis=2)
    )
    return (picker, merge_lookup)


def expert_terms(piece, w_gate, w_up, w_down):
    outputs = []
    for local in range(w_gate.shape[0]):
        rows = piece[:, :, local].reshape(-1, piece.shape[-1])
        gate_value = jnp.einsum(
            "md,fd->mf", rows, w_gate[local], preferred_element_type=jnp.float32
        )
        up_value = jnp.einsum("md,fd->mf", rows, w_up[local], preferred_element_type=jnp.float32)
        hidden = (jax.nn.silu(gate_value) * up_value).astype(jnp.bfloat16)
        result = jnp.dot(hidden, w_down[local], preferred_element_type=jnp.float32)
        outputs.append(
            result.reshape(piece.shape[0], piece.shape[1], piece.shape[3], piece.shape[4])
        )
    return jnp.stack(outputs, axis=2)


def experts(moe_input, routes, route_weight, w_gate, w_up, w_down):
    groups = lax.axis_size("exp")
    local_count = w_gate.shape[0]
    row_total = moe_input.shape[0]
    capacity = max(2, row_total // 2)
    picker, merge_lookup = route_tables(routes, route_weight, groups * local_count, capacity)
    departing_memory = jnp.dot(
        picker.astype(jnp.bfloat16), moe_input, preferred_element_type=jnp.float32
    ).astype(jnp.bfloat16)
    departing_memory = departing_memory.reshape(groups, local_count, capacity, moe_input.shape[1])
    arrived = lax.all_to_all(departing_memory, "exp", split_axis=0, concat_axis=0, tiled=True)
    gathered = lax.all_gather(arrived[None], "ctx", axis=0, tiled=True)
    terms = expert_terms(gathered, w_gate, w_up, w_down)
    summed = lax.psum_scatter(
        terms.astype(jnp.bfloat16), "ctx", scatter_dimension=0, tiled=True
    ).astype(jnp.float32)
    finished = summed[0].astype(jnp.bfloat16)
    returned = lax.all_to_all(finished, "exp", split_axis=0, concat_axis=0, tiled=True)
    returned = returned.reshape(groups * local_count * capacity, moe_input.shape[1])
    mixed = jnp.dot(merge_lookup.T, returned.astype(jnp.float32), precision=lax.Precision.HIGHEST)
    return mixed.astype(jnp.bfloat16)


def body(
    queries,
    attn_keys,
    attn_values,
    out_grad,
    log_decay,
    moe_input,
    routes,
    route_weight,
    w_gate,
    w_up,
    w_down,
):
    attention_parts = attention(queries, attn_keys, attn_values, out_grad, log_decay)
    moe_out = experts(moe_input, routes, route_weight, w_gate, w_up, w_down)
    return attention_parts + (moe_out,)


def solution(mesh):
    placed = (
        P("ctx", "exp"),
        P("ctx", "exp"),
        P("ctx", "exp"),
        P("ctx", "exp"),
        P("ctx", "exp"),
        P(("ctx", "exp"), None),
        P(("ctx", "exp"), None),
        P(("ctx", "exp"), None),
        P("exp", "ctx", None),
        P("exp", "ctx", None),
        P("exp", "ctx", None),
    )
    return jax.shard_map(
        body,
        mesh=mesh,
        in_specs=placed,
        out_specs=(
            P("ctx", "exp"),
            P("ctx", "exp"),
            P("ctx", "exp"),
            P("ctx", "exp"),
            P(("ctx", "exp"), None),
        ),
        check_vma=False,
    )
```

profile of v0, /device:TPU:0, one launch (start us, length us, event | category | flops | bytes accessed | tf_op | source)
XLA Modules:
  0.0 465.3 jit_solution(8278910734743402851)
XLA Ops:
  7.3 0.8 copy.166
  10.2 1.3 convolution_convert_fusion
  11.5 15.8 %all_to_all.10 = bf16[4,2,16,3072]{3,2,1,0:T(8,128)(2,1)} all-to-all(bf16[4,2,16,3072]{3,2,1,0:T(8,128)(2,1)S(1)} %bitcast.199), channel_id=1, replica_groups=mesh['ctx'=8,'exp'=4] {'exp'}, dimensions={0} | all-to-all | bytes 1572864 | tf_op jit(solution)/shard_map/all_to_all | solution.py:157
  28.0 1.1 convolution_convert_fusion.3
  29.6 1.4 convolution_convert_fusion.2
  31.8 21.9 %all-gather.3 = bf16[8,1,8]{2,1,0:T(2,128)(2,1)S(1)} all-gather(bf16[1,1,8]{2,1,0:T(2,128)(2,1)S(1)} %get-tuple-element.321), channel_id=1, replica_groups=mesh['ctx'=8,'exp'=4] {'ctx'}, dimensions={0}, use_global_device_ids=true | all-gather | bytes 144 | tf_op jit(solution)/shard_map/all_gather | solution.py:10
  54.4 72.6 %all-gather.12.cloned.1.call-done = bf16[32,2,16,3072]{3,2,1,0:T(8,128)(2,1)} async-done(((bf16[4,2,16,3072]{3,2,1,0:T(8,128)(2,1)}), bf16[32,2,16,3072]{3,2,1,0:T(8,128)(2,1)}) %all-gather.12.cloned.1.call-update) | async-done | bytes 6291472 | tf_op jit(solution)/shard_map/all_gather | solution.py:158
  127.0 3.5 fusion.74
  130.5 8.7 %fusion.8 = f32[512,1152]{1,0:T(8,128)} fusion(bf16[512,3072]{1,0:T(8,128)(2,1)S(1)} %bitcast.202, bf16[2,1152,3072]{2,1,0:T(8,128)(2,1)} %param.23), kind=kOutput, calls=%fused_computation.12 | convolution fusion | flops 3623878656 | bytes 12582912 | tf_op jit(solution)/shard_map/md,fd->mf/dot_general | solution.py:135
  139.2 5.7 %fusion.12 = f32[512,1152]{1,0:T(8,128)} fusion(bf16[512,3072]{1,0:T(8,128)(2,1)S(1)} %bitcast.200, bf16[2,1152,3072]{2,1,0:T(8,128)(2,1)S(1)} %bitcast.213), kind=kOutput, calls=%fused_computation.16 | convolution fusion | flops 3623878656 | bytes 12582912 | tf_op jit(solution)/shard_map/md,fd->mf/dot_general | solution.py:135
  144.9 8.1 %fusion.38 = bf16[512,1152]{1,0:T(8,128)(2,1)S(1)} fusion(bf16[512,3072]{1,0:T(8,128)(2,1)S(1)} %bitcast.203, bf16[2,1152,3072]{2,1,0:T(8,128)(2,1)} %param.24, f32[512,1152]{1,0:T(8,128)} %fusion.8), kind=kOutput, calls=%fused_computation.33 | convolution fusion | flops 3627417600 | bytes 13762560 | tf_op jit(solution)/shard_map/md,fd->mf/dot_general | solution.py:138
  153.1 7.6 %fusion.41 = bf16[512,1152]{1,0:T(8,128)(2,1)S(1)} fusion(bf16[512,3072]{1,0:T(8,128)(2,1)S(1)} %bitcast.201, bf16[2,1152,3072]{2,1,0:T(8,128)(2,1)} %param.24, f32[512,1152]{1,0:T(8,128)S(1)} %copy-done.8), kind=kOutput, calls=%fused_computation.34 | convolution fusion | flops 3627417600 | bytes 13762560 | tf_op jit(solution)/shard_map/md,fd->mf/dot_general | solution.py:138
  160.6 7.6 %fusion.26 = bf16[8,4,1,16,3072]{4,3,1,0,2:T(8,128)(2,1)S(1)} fusion(bf16[8,4,16,1152]{3,2,1,0:T(8,128)(2,1)S(1)} %bitcast.214, bf16[2,1152,3072]{2,1,0:T(8,128)(2,1)} %param.25), kind=kOutput, calls=%fused_computation.27 | convolution fusion | flops 3625451520 | bytes 11403264 | tf_op jit(solution)/shard_map/dot_general | solution.py:140
  168.3 7.8 %fusion.29 = bf16[8,4,1,16,3072]{4,3,1,0,2:T(8,128)(2,1)S(1)} fusion(bf16[8,4,16,1152]{3,2,1,0:T(8,128)(2,1)S(1)} %bitcast.215, bf16[2,1152,3072]{2,1,0:T(8,128)(2,1)} %param.25), kind=kOutput, calls=%fused_computation.28 | convolution fusion | flops 3625451520 | bytes 11403264 | tf_op jit(solution)/shard_map/dot_general | solution.py:140
  176.0 3.2 pad_maximum_fusion
  179.2 9.1 %while.30 = (s32[]{:T(128)}, f32[8,128,128]{2,1,0:T(8,128)S(1)}, s32[]{:T(128)}, bf16[8,8]{1,0:T(8,128)(2,1)S(1)}, bf16[8,8,128,128]{3,2,1,0:T(8,128)(2,1)}, /*index=5*/s32[]{:T(128)}, s32[]{:T(128)}) while((s32[]{:T(128)}, f32[8,128,128]{2,1,0:T(8,128)S(1)}, s32[]{:T(128)}, bf16[8,8]{1,0:T(8,128)(2,1)S(1)}, ...), condition=%wide.region_2.3_spmd.clone, body=%wide.region_1.2_spmd.clone.sunk | while | flops 655372 | bytes 1310913 | solution.py:28
  179.3 1.1 fusion.108
  180.4 1.1 fusion.108
  181.5 1.1 fusion.108
  182.7 1.1 fusion.108
  183.8 1.1 fusion.108
  185.0 1.1 fusion.108
  186.1 1.1 fusion.108
  187.2 1.1 fusion.108
  189.0 1.0 fusion.54
  190.0 37.3 %all-gather.10.cloned.1.call-done = bf16[64,128,128]{2,1,0:T(8,128)(2,1)} async-done(((bf16[8,128,128]{2,1,0:T(8,128)(2,1)}), bf16[64,128,128]{2,1,0:T(8,128)(2,1)}) %all-gather.10.cloned.1.call-update) | async-done | bytes 2097168 | tf_op jit(solution)/shard_map/all_gather | solution.py:10
  227.3 9.2 %while.31 = (s32[]{:T(128)}, f32[8,128,128]{2,1,0:T(8,128)S(1)}, s32[]{:T(128)}, bf16[8,8]{1,0:T(8,128)(2,1)S(1)}, bf16[8,8,128,128]{3,2,1,0:T(8,128)(2,1)}, /*index=5*/s32[]{:T(128)}, s32[]{:T(128)}, s32[]{:T(128)}, s32[]{:T(128)}) while((s32[]{:T(128)}, f32[8,128,128]{2,1,0:T(8,128)S(1)}, s32[]{:T(128)}, ...), condition=%wide.region_4.5_spmd.clone, body=%wide.region_3.4_spmd.clone.sunk | while | flops 655376 | bytes 1310975 | solution.py:28
  227.3 1.1 fusion.109
  228.5 1.1 fusion.109
  229.6 1.1 fusion.109
  230.8 1.1 fusion.109
  231.9 1.1 fusion.109
  233.0 1.1 fusion.109
  234.2 1.2 fusion.109
  235.4 1.1 fusion.109
  237.2 1.0 fusion.53
  238.1 1.0 convolution_bitcast_fusion.7
  239.2 200.7 %all-reduce.3.cloned.1.call-done = bf16[8,4,2,16,3072]{4,3,1,0,2:T(8,128)(2,1)} async-done(((bf16[8,4,2,16,3072]{4,3,1,0,2:T(8,128)(2,1)}), bf16[8,4,2,16,3072]{4,3,1,0,2:T(8,128)(2,1)}) %all-reduce.3.cloned.1.call-update) | async-done | bytes 6291472
  439.8 1.8 dynamic-slice_bitcast_fusion
  441.7 1.0 copy.168
  442.6 3.5 all-to-all-start.1
  446.1 1.0 fusion.55
  447.2 1.8 copy.169
  448.9 0.8 copy.170
  449.8 0.8 copy.171
  451.5 0.8 copy.172
  452.3 5.4 %all-to-all-done.1 = bf16[4,2,16,3072]{3,2,1,0:T(8,128)(2,1)S(1)} async-done(((bf16[4,2,16,3072]{3,2,1,0:T(8,128)(2,1)}), bf16[4,2,16,3072]{3,2,1,0:T(8,128)(2,1)S(1)}, u32[]{:S(2)}, u32[]{:S(2)}) %all-to-all-start.1) | async-done | bytes 786464 | tf_op jit(solution)/shard_map/all_to_all | solution.py:164
  457.7 1.1 convolution_convert_fusion.1
  (81 shorter events, 6.9 us)
Async XLA Ops:
  7.2 20.8 %copy-start = (bf16[128,1024]{1,0:T(8,128)(2,1)S(1)}, bf16[128,1024]{1,0:T(8,128)(2,1)}, u32[]{:S(2)}) copy-start(bf16[128,1024]{1,0:T(8,128)(2,1)} %param.17) | copy-start | bytes 786436
  7.2 20.2 %copy-start.6 = (f32[128,8]{0,1:T(8,128)S(1)}, f32[128,8]{0,1:T(8,128)}, u32[]{:S(2)}) copy-start(f32[128,8]{0,1:T(8,128)} %param.19) | copy-start | bytes 12292
  7.2 20.3 %copy-start.3 = (bf16[128,1024]{1,0:T(8,128)(2,1)S(1)}, bf16[128,1024]{1,0:T(8,128)(2,1)}, u32[]{:S(2)}) copy-start(bf16[128,1024]{1,0:T(8,128)(2,1)} %param.16) | copy-start | bytes 786436
  7.2 22.0 %copy-start.4 = (bf16[128,1024]{1,0:T(8,128)(2,1)S(1)}, bf16[128,1024]{1,0:T(8,128)(2,1)}, u32[]{:S(2)}) copy-start(bf16[128,1024]{1,0:T(8,128)(2,1)} %param.15) | copy-start | bytes 786436
  7.2 22.2 %copy-start.5 = (bf16[128,1024]{1,0:T(8,128)(2,1)S(1)}, bf16[128,1024]{1,0:T(8,128)(2,1)}, u32[]{:S(2)}) copy-start(bf16[128,1024]{1,0:T(8,128)(2,1)} %param.18) | copy-start | bytes 786436
  7.2 119.8 %all-gather.12.cloned.1.call-start = ((), (), s32[]{:S(2)}) async-start(), calls=%async_computation.4 | async-start | bytes 7077888 | tf_op jit(solution)/shard_map/all_gather | solution.py:158
  27.3 151.9 %all-gather.8.cloned.1.call-start = ((), (), s32[]{:S(2)}) async-start(), calls=%async_computation.2 | async-start | bytes 2359296 | tf_op jit(solution)/shard_map/all_gather | solution.py:10
  27.9 25.9 %copy-start.7 = (u32[32]{0:T(128)S(1)}, u32[32]{0:T(128)}, u32[]{:S(2)}) copy-start(u32[32]{0:T(128)} %constant.94) | copy-start | bytes 388
  29.1 198.2 %all-gather.10.cloned.1.call-start = ((), (), s32[]{:S(2)}) async-start(), calls=%async_computation.3 | async-start | bytes 2359296 | tf_op jit(solution)/shard_map/all_gather | solution.py:10
  31.0 408.8 %all-reduce.3.cloned.1.call-start = ((), (), s32[]{:S(2)}) async-start(), calls=%async_computation.5 | async-start | bytes 12582912
  127.0 12.2 %slice-start = ((s8[14155776]{0:T(1024)(128)(4,1)}), s8[4194304]{0:T(1024)(128)(4,1)S(1)}, s32[]{:S(2)}) async-start(s8[14155776]{0:T(1024)(128)(4,1)} %bitcast.212), calls=%async_computation.6 | async-start | bytes 8388608
  127.0 12.2 %slice-start.1 = ((s8[14155776]{0:T(1024)(128)(4,1)}), s8[4194304]{0:T(1024)(128)(4,1)S(1)}, s32[]{:S(2)}) async-start(s8[14155776]{0:T(1024)(128)(4,1)} %bitcast.212), calls=%async_computation.7 | async-start | bytes 8388608
  130.5 8.7 %slice-start.2 = ((s8[14155776]{0:T(1024)(128)(4,1)}), s8[4194304]{0:T(1024)(128)(4,1)S(1)}, s32[]{:S(2)}) async-start(s8[14155776]{0:T(1024)(128)(4,1)} %bitcast.212), calls=%async_computation.8 | async-start | bytes 8388608
  130.5 8.7 %slice-start.3 = ((s8[14155776]{0:T(1024)(128)(4,1)}), s8[1572864]{0:T(1024)(128)(4,1)S(1)}, s32[]{:S(2)}) async-start(s8[14155776]{0:T(1024)(128)(4,1)} %bitcast.212), calls=%async_computation.9 | async-start | bytes 3145728
  144.9 8.1 %copy-start.8 = (f32[512,1152]{1,0:T(8,128)S(1)}, f32[512,1152]{1,0:T(8,128)}, u32[]{:S(2)}) copy-start(f32[512,1152]{1,0:T(8,128)} %fusion.12) | copy-start | bytes 7077892
  439.8 9.1 %copy-start.1 = (bf16[128,8,128]{0,2,1:T(8,128)(2,1)S(1)}, bf16[128,8,128]{0,2,1:T(8,128)(2,1)}, u32[]{:S(2)}) copy-start(bf16[128,8,128]{0,2,1:T(8,128)(2,1)} %fusion.54) | copy-start | bytes 786436
  441.6 8.2 %copy-start.2 = (bf16[128,8,128]{0,2,1:T(8,128)(2,1)S(1)}, bf16[128,8,128]{0,2,1:T(8,128)(2,1)}, u32[]{:S(2)}) copy-start(bf16[128,8,128]{0,2,1:T(8,128)(2,1)} %fusion.53) | copy-start | bytes 786436
  442.6 15.1 %all-to-all-start.1 = ((bf16[4,2,16,3072]{3,2,1,0:T(8,128)(2,1)}), bf16[4,2,16,3072]{3,2,1,0:T(8,128)(2,1)S(1)}, u32[]{:S(2)}, u32[]{:S(2)}) async-start(bf16[4,2,16,3072]{3,2,1,0:T(8,128)(2,1)} %copy.168), calls=%async_computation.1 | async-start | bytes 1572864 | tf_op jit(solution)/shard_map/all_to_all | solution.py:164
Sparse Core Ops, SparseCore 0:
  27.4 99.4 all-gather.11
  129.7 47.2 all-gather.7
  179.7 47.5 all-gather.9
  231.0 208.8 all-reduce.2
where the time goes:
time: 466 us; the launch traced here: 465 us
  waiting for transfers between devices  316 us (68%)
  matrix products  57.2 us (12%)
  blocking collectives  37.7 us (8%)
  other arithmetic  22.9 us (5%)
  between operations  14.1 us (3%)
  local copies, waits for them, and re-layouts  13.2 us (3%)
    unnamed x5, waiting for transfers between devices  201 us
    all_gather x1, waiting for transfers between devices, experts(): gathered = lax.all_gather(arrived[None], 'ctx', axis=0, tiled=True)  72.6 us
    all_gather x2, waiting for transfers between devices, entering(): lax.all_gather(part.astype(kind), axis)  37.3 us
    all_gather x1, blocking collectives, entering(): lax.all_gather(part.astype(kind), axis)  21.9 us
    select_n x16, other arithmetic, step(): return jax.tree.map(lambda a, b: jnp.where(reached, a, b), new, before)  17.6 us
    all_to_all x1, blocking collectives, experts(): lax.all_to_all(departing_memory, 'exp', split_axis=0, concat_axis=0, tile...  15.8 us
    dot_general x2, matrix products, expert_terms(): jnp.einsum('md,fd->mf', rows, w_up[local], preferred_element_type=jnp.flo...  15.7 us
    dot_general x2, matrix products, expert_terms(): result = jnp.dot(hidden, w_down[local], preferred_element_type=jnp.float32)  15.4 us
  transfers between devices with their start and end apart: 5, of which 4 were waited for; matrix products, arithmetic and copies ran while one was open for 18% of the time, Pallas kernels for 0%

commit v1 on v0

--- a/solution.py
+++ b/solution.py
@@ -2,6 +2,7 @@
 import jax.numpy as jnp
 from jax import lax
 from jax.sharding import PartitionSpec as P
+from jax.lax import axis_index, axis_size, ppermute
 
 
 def entering(value, axis, combine, identity, reverse):
@@ -155,7 +156,16 @@
     ).astype(jnp.bfloat16)
     departing_memory = departing_memory.reshape(groups, local_count, capacity, moe_input.shape[1])
     arrived = lax.all_to_all(departing_memory, "exp", split_axis=0, concat_axis=0, tiled=True)
-    gathered = lax.all_gather(arrived[None], "ctx", axis=0, tiled=True)
+    g_now = arrived[None]
+    n_all = axis_size("ctx")
+    sheets = [g_now]
+    block_next = [(hop_no - 1, hop_no) for hop_no in range(1, n_all)] + [(n_all - 1, 0)]
+    for _ in range(n_all - 1):
+        g_now = ppermute(g_now, axis_name="ctx", perm=block_next)
+        sheets += [g_now]
+    v_now = jnp.concatenate([*reversed(sheets)], axis=0)
+    b_now = axis_index("ctx")
+    gathered = jnp.roll(v_now, (b_now + 1) * g_now.shape[0], axis=0)
     terms = expert_terms(gathered, w_gate, w_up, w_down)
     summed = lax.psum_scatter(
         terms.astype(jnp.bfloat16), "ctx", scatter_dimension=0, tiled=True

time: 466 us -> 486 us (1.043)
  local copies, waits for them, and re-layouts: 13.2 us -> 24 us
  waiting for transfers between devices: 316 us -> 326 us
    ppermute x0 -> x7, waiting for transfers between devices: none -> 134 us  [experts(): g_now = ppermute(g_now, axis_name='ctx', perm=block_next)]
    all_gather x1 -> x0, waiting for transfers between devices: 72.6 us -> none  [experts(): gathered = lax.all_gather(arrived[None], 'ctx', axis=0, tiled=True)]
    all_gather x2, waiting for transfers between devices: 37.3 us -> 0.02 us  [entering(): lax.all_gather(part.astype(kind), axis)]
    unnamed x5 -> x4, waiting for transfers between devices: 201 us -> 186 us
    unnamed x35 -> x46, local copies, waits for them, and re-layouts: 6.1 us -> 17.4 us
  transfers between devices with their start and end apart: 5 -> 11, of which waited for: 4 -> 8; matrix products, arithmetic and copies ran while one was open for 18% -> 19% of each run, Pallas kernels for 0% -> 0%
where the time goes in v1:
time: 486 us; the launch traced here: 485 us
  waiting for transfers between devices  326 us (67%)
  matrix products  54 us (11%)
  blocking collectives  38.7 us (8%)
  local copies, waits for them, and re-layouts  24 us (5%)
  other arithmetic  22.8 us (5%)
  between operations  14.2 us (3%)
  starting transfers between devices  5.14 us (1%)
    unnamed x4, waiting for transfers between devices  186 us
    ppermute x7, waiting for transfers between devices, experts(): g_now = ppermute(g_now, axis_name='ctx', perm=block_next)  134 us
    all_gather x1, blocking collectives, entering(): lax.all_gather(part.astype(kind), axis)  23 us
    select_n x16, other arithmetic, step(): return jax.tree.map(lambda a, b: jnp.where(reached, a, b), new, before)  17.5 us
    unnamed x46, local copies, waits for them, and re-layouts  17.4 us
    all_to_all x1, blocking collectives, experts(): lax.all_to_all(departing_memory, 'exp', split_axis=0, concat_axis=0, tile...  15.7 us
    dot_general x2, matrix products, expert_terms(): result = jnp.dot(hidden, w_down[local], preferred_element_type=jnp.float32)  15.3 us
    dot_general x2, matrix products, expert_terms(): jnp.einsum('md,fd->mf', rows, w_up[local], preferred_element_type=jnp.flo...  14.6 us
  transfers between devices with their start and end apart: 11, of which 8 were waited for; matrix products, arithmetic and copies ran while one was open for 19% of the time, Pallas kernels for 0%

profile of v1, /device:TPU:0, one launch (start us, length us, event | category | flops | bytes accessed | tf_op | source)
XLA Modules:
  0.0 485.1 jit_solution(6574316420265048099)
XLA Ops:
  10.1 1.3 convolution_convert_fusion
  11.5 15.7 %all_to_all.10 = bf16[4,2,16,3072]{3,2,1,0:T(8,128)(2,1)S(1)} all-to-all(bf16[4,2,16,3072]{3,2,1,0:T(8,128)(2,1)S(1)} %bitcast.201), channel_id=1, replica_groups=mesh['ctx'=8,'exp'=4] {'exp'}, dimensions={0} | all-to-all | bytes 1572864 | tf_op jit(solution)/shard_map/all_to_all | solution.py:158
  27.1 1.5 collective-permute-start
  29.6 19.3 %collective-permute-done = bf16[1,4,2,16,3072]{4,3,2,1,0:T(8,128)(2,1)S(1)} collective-permute-done((bf16[1,4,2,16,3072]{4,3,2,1,0:T(8,128)(2,1)S(1)}, bf16[1,4,2,16,3072]{4,3,2,1,0:T(8,128)(2,1)S(1)}, u32[]{:S(2)}, u32[]{:S(2)}) %collective-permute-start) | collective-permute-done | bytes 786464 | tf_op jit(solution)/shard_map/ppermute | solution.py:164
  49.0 1.3 copy.184
  50.3 1.1 copy.185
  51.4 1.4 convolution_convert_fusion.2
  52.9 22.1 %collective-permute-done.1 = bf16[1,4,2,16,3072]{4,3,2,1,0:T(8,128)(2,1)S(1)} collective-permute-done((bf16[1,4,2,16,3072]{4,3,2,1,0:T(8,128)(2,1)S(1)}, bf16[1,4,2,16,3072]{4,3,2,1,0:T(8,128)(2,1)S(1)}, u32[]{:S(2)}, u32[]{:S(2)}) %collective-permute-start.1) | collective-permute-done | bytes 786464 | tf_op jit(solution)/shard_map/ppermute | solution.py:164
  75.0 20.0 %collective-permute-done.2 = bf16[1,4,2,16,3072]{4,3,2,1,0:T(8,128)(2,1)S(1)} collective-permute-done((bf16[1,4,2,16,3072]{4,3,2,1,0:T(8,128)(2,1)S(1)}, bf16[1,4,2,16,3072]{4,3,2,1,0:T(8,128)(2,1)S(1)}, u32[]{:S(2)}, u32[]{:S(2)}) %collective-permute-start.2) | collective-permute-done | bytes 786464 | tf_op jit(solution)/shard_map/ppermute | solution.py:164
  95.9 37.2 %collective-permute-done.3 = bf16[1,4,2,16,3072]{4,3,2,1,0:T(8,128)(2,1)S(1)} collective-permute-done((bf16[1,4,2,16,3072]{4,3,2,1,0:T(8,128)(2,1)S(1)}, bf16[1,4,2,16,3072]{4,3,2,1,0:T(8,128)(2,1)S(1)}, u32[]{:S(2)}, u32[]{:S(2)}) %collective-permute-start.3) | collective-permute-done | bytes 786464 | tf_op jit(solution)/shard_map/ppermute | solution.py:164
  134.0 17.5 %collective-permute-done.4 = bf16[1,4,2,16,3072]{4,3,2,1,0:T(8,128)(2,1)} collective-permute-done((bf16[1,4,2,16,3072]{4,3,2,1,0:T(8,128)(2,1)S(1)}, bf16[1,4,2,16,3072]{4,3,2,1,0:T(8,128)(2,1)}, u32[]{:S(2)}, u32[]{:S(2)}) %collective-permute-start.4) | collective-permute-done | bytes 786464 | tf_op jit(solution)/shard_map/ppermute | solution.py:164
  151.6 1.1 copy.143
  152.7 17.5 %collective-permute-done.5 = bf16[1,4,2,16,3072]{4,3,2,1,0:T(8,128)(2,1)} collective-permute-done((bf16[1,4,2,16,3072]{4,3,2,1,0:T(8,128)(2,1)}, bf16[1,4,2,16,3072]{4,3,2,1,0:T(8,128)(2,1)}, u32[]{:S(2)}, u32[]{:S(2)}) %collective-permute-start.5) | collective-permute-done | bytes 786464 | tf_op jit(solution)/shard_map/ppermute | solution.py:164
  170.2 1.1 convolution_convert_fusion.3
  171.4 23.0 %all-gather.2 = bf16[8,1,8]{2,1,0:T(2,128)(2,1)S(1)} all-gather(bf16[1,1,8]{2,1,0:T(2,128)(2,1)S(1)} %get-tuple-element.321), channel_id=1, replica_groups=mesh['ctx'=8,'exp'=4] {'ctx'}, dimensions={0}, use_global_device_ids=true | all-gather | bytes 144 | tf_op jit(solution)/shard_map/all_gather | solution.py:11
  195.9 1.2 constant_dynamic-update-slice_fusion.15
  197.1 1.2 constant_dynamic-update-slice_fusion.14
  198.3 1.4 constant_dynamic-update-slice_fusion.13
  200.0 1.2 constant_dynamic-update-slice_fusion.7
  201.2 1.2 constant_dynamic-update-slice_fusion.6
  202.4 1.2 constant_dynamic-update-slice_fusion.5
  204.7 6.7 %fusion.12 = f32[512,1152]{1,0:T(8,128)S(1)} fusion(bf16[512,3072]{1,0:T(8,128)(2,1)S(1)} %bitcast.204, bf16[2,1152,3072]{2,1,0:T(8,128)(2,1)} %param.23), kind=kOutput, calls=%fused_computation.16 | convolution fusion | flops 3623878656 | bytes 12582912 | tf_op jit(solution)/shard_map/md,fd->mf/dot_general | solution.py:136
  211.4 6.5 %fusion.8 = f32[512,1152]{1,0:T(8,128)S(1)} fusion(bf16[512,3072]{1,0:T(8,128)(2,1)S(1)} %bitcast.202, bf16[2,1152,3072]{2,1,0:T(8,128)(2,1)} %param.23), kind=kOutput, calls=%fused_computation.12 | convolution fusion | flops 3623878656 | bytes 12582912 | tf_op jit(solution)/shard_map/md,fd->mf/dot_general | solution.py:136
  218.0 7.3 %fusion.41 = bf16[512,1152]{1,0:T(8,128)(2,1)S(1)} fusion(bf16[512,3072]{1,0:T(8,128)(2,1)S(1)} %bitcast.205, bf16[2,1152,3072]{2,1,0:T(8,128)(2,1)} %param.24, f32[512,1152]{1,0:T(8,128)S(1)} %fusion.12), kind=kOutput, calls=%fused_computation.34 | convolution fusion | flops 3627417600 | bytes 13762560 | tf_op jit(solution)/shard_map/md,fd->mf/dot_general | solution.py:139
  225.3 7.3 %fusion.38 = bf16[512,1152]{1,0:T(8,128)(2,1)S(1)} fusion(bf16[512,3072]{1,0:T(8,128)(2,1)S(1)} %bitcast.203, bf16[2,1152,3072]{2,1,0:T(8,128)(2,1)} %param.24, f32[512,1152]{1,0:T(8,128)S(1)} %fusion.8), kind=kOutput, calls=%fused_computation.33 | convolution fusion | flops 3627417600 | bytes 13762560 | tf_op jit(solution)/shard_map/md,fd->mf/dot_general | solution.py:139
  232.6 7.6 %fusion.29 = bf16[8,4,1,16,3072]{4,3,1,0,2:T(8,128)(2,1)S(1)} fusion(bf16[8,4,16,1152]{3,2,1,0:T(8,128)(2,1)S(1)} %bitcast.214, bf16[2,1152,3072]{2,1,0:T(8,128)(2,1)} %param.25), kind=kOutput, calls=%fused_computation.28 | convolution fusion | flops 3625451520 | bytes 11403264 | tf_op jit(solution)/shard_map/dot_general | solution.py:141
  240.2 7.7 %fusion.26 = bf16[8,4,1,16,3072]{4,3,1,0,2:T(8,128)(2,1)S(1)} fusion(bf16[8,4,16,1152]{3,2,1,0:T(8,128)(2,1)S(1)} %bitcast.215, bf16[2,1152,3072]{2,1,0:T(8,128)(2,1)} %param.25), kind=kOutput, calls=%fused_computation.27 | convolution fusion | flops 3625451520 | bytes 11403264 | tf_op jit(solution)/shard_map/dot_general | solution.py:141
  247.9 3.2 pad_maximum_fusion
  251.1 9.2 %while.31 = (s32[]{:T(128)}, f32[8,128,128]{2,1,0:T(8,128)S(1)}, s32[]{:T(128)}, bf16[8,8]{1,0:T(8,128)(2,1)S(1)}, bf16[8,8,128,128]{3,2,1,0:T(8,128)(2,1)}, /*index=5*/s32[]{:T(128)}, s32[]{:T(128)}, s32[]{:T(128)}, s32[]{:T(128)}) while((s32[]{:T(128)}, f32[8,128,128]{2,1,0:T(8,128)S(1)}, s32[]{:T(128)}, ...), condition=%wide.region_4.5_spmd.clone, body=%wide.region_3.4_spmd.clone.sunk | while | flops 655376 | bytes 1310967 | solution.py:29
  251.1 1.1 fusion.108
  252.3 1.1 fusion.108
  253.4 1.1 fusion.108
  254.6 1.1 fusion.108
  255.7 1.1 fusion.108
  256.9 1.1 fusion.108
  258.0 1.1 fusion.108
  259.2 1.1 fusion.108
  261.9 9.0 %while.30 = (s32[]{:T(128)}, f32[8,128,128]{2,1,0:T(8,128)S(1)}, s32[]{:T(128)}, bf16[8,8]{1,0:T(8,128)(2,1)S(1)}, bf16[8,8,128,128]{3,2,1,0:T(8,128)(2,1)}, /*index=5*/s32[]{:T(128)}, s32[]{:T(128)}) while((s32[]{:T(128)}, f32[8,128,128]{2,1,0:T(8,128)S(1)}, s32[]{:T(128)}, bf16[8,8]{1,0:T(8,128)(2,1)S(1)}, ...), condition=%wide.region_2.3_spmd.clone, body=%wide.region_1.2_spmd.clone.sunk | while | flops 655372 | bytes 1310905 | solution.py:29
  261.9 1.1 fusion.107
  263.0 1.1 fusion.107
  264.1 1.1 fusion.107
  267.5 1.1 fusion.107
  273.2 186.3 %all-reduce.3.cloned.1.call-done = bf16[8,4,2,16,3072]{4,3,1,0,2:T(8,128)(2,1)} async-done(((bf16[8,4,2,16,3072]{4,3,1,0,2:T(8,128)(2,1)}), bf16[8,4,2,16,3072]{4,3,1,0,2:T(8,128)(2,1)}) %all-reduce.3.cloned.1.call-update) | async-done | bytes 6291472
  459.5 1.9 dynamic-slice_bitcast_fusion
  462.3 3.5 all-to-all-start.1
  466.9 1.8 copy.171
  471.7 5.7 %all-to-all-done.1 = bf16[4,2,16,3072]{3,2,1,0:T(8,128)(2,1)S(1)} async-done(((bf16[4,2,16,3072]{3,2,1,0:T(8,128)(2,1)}), bf16[4,2,16,3072]{3,2,1,0:T(8,128)(2,1)S(1)}, u32[]{:S(2)}, u32[]{:S(2)}) %all-to-all-start.1) | async-done | bytes 786464 | tf_op jit(solution)/shard_map/all_to_all | solution.py:174
  477.4 1.1 convolution_convert_fusion.1
  (103 shorter events, 22.2 us)
Async XLA Ops:
  7.2 163.0 %copy-start = (bf16[128,1024]{1,0:T(8,128)(2,1)S(1)}, bf16[128,1024]{1,0:T(8,128)(2,1)}, u32[]{:S(2)}) copy-start(bf16[128,1024]{1,0:T(8,128)(2,1)} %param.17) | copy-start | bytes 786436
  7.2 187.3 %copy-start.10 = (u32[32]{0:T(128)S(1)}, u32[32]{0:T(128)}, u32[]{:S(2)}) copy-start(u32[32]{0:T(128)} %constant.117) | copy-start | bytes 388
  7.2 243.9 %all-gather.8.cloned.1.call-start = ((), (), s32[]{:S(2)}) async-start(), calls=%async_computation.3 | async-start | bytes 2359296 | tf_op jit(solution)/shard_map/all_gather | solution.py:11
  27.1 21.7 %collective-permute-start = (bf16[1,4,2,16,3072]{4,3,2,1,0:T(8,128)(2,1)S(1)}, bf16[1,4,2,16,3072]{4,3,2,1,0:T(8,128)(2,1)S(1)}, u32[]{:S(2)}, u32[]{:S(2)}) collective-permute-start(bf16[1,4,2,16,3072]{4,3,2,1,0:T(8,128)(2,1)S(1)} %bitcast.187), channel_id=1, source_target_pairs={{0,4},{4,8},{8,12},{12,16},{16,20},{20,24},{24,28},{28,0},{1,5},{5... | collective-permute-start | bytes 2359304 | tf_op jit(solution)/shard_map/ppermute | solution.py:164
  48.9 122.5 %copy-start.1 = (bf16[1,4,2,16,3072]{4,3,2,1,0:T(8,128)(2,1)}, bf16[1,4,2,16,3072]{4,3,2,1,0:T(8,128)(2,1)S(1)}, u32[]{:S(2)}) copy-start(bf16[1,4,2,16,3072]{4,3,2,1,0:T(8,128)(2,1)S(1)} %collective-permute-done) | copy-start | bytes 2359300
  48.9 26.1 %collective-permute-start.1 = (bf16[1,4,2,16,3072]{4,3,2,1,0:T(8,128)(2,1)S(1)}, bf16[1,4,2,16,3072]{4,3,2,1,0:T(8,128)(2,1)S(1)}, u32[]{:S(2)}, u32[]{:S(2)}) collective-permute-start(bf16[1,4,2,16,3072]{4,3,2,1,0:T(8,128)(2,1)S(1)} %collective-permute-done), channel_id=1, source_target_pairs={{0,4},{4,8},{8,12},{12,16},{16,20},{20,24},{24,28},{28,0},{1,5},{5... | collective-permute-start | bytes 2359304 | tf_op jit(solution)/shard_map/ppermute | solution.py:164
  52.8 209.0 %all-gather.6.cloned.1.call-start = ((), (), s32[]{:S(2)}) async-start(), calls=%async_computation.2 | async-start | bytes 2359296 | tf_op jit(solution)/shard_map/all_gather | solution.py:11
  75.0 76.5 %copy-start.3 = (bf16[1,4,2,16,3072]{4,3,2,1,0:T(8,128)(2,1)}, bf16[1,4,2,16,3072]{4,3,2,1,0:T(8,128)(2,1)S(1)}, u32[]{:S(2)}) copy-start(bf16[1,4,2,16,3072]{4,3,2,1,0:T(8,128)(2,1)S(1)} %collective-permute-done.1) | copy-start | bytes 2359300
  75.0 20.0 %collective-permute-start.2 = (bf16[1,4,2,16,3072]{4,3,2,1,0:T(8,128)(2,1)S(1)}, bf16[1,4,2,16,3072]{4,3,2,1,0:T(8,128)(2,1)S(1)}, u32[]{:S(2)}, u32[]{:S(2)}) collective-permute-start(bf16[1,4,2,16,3072]{4,3,2,1,0:T(8,128)(2,1)S(1)} %collective-permute-done.1), channel_id=1, source_target_pairs={{0,4},{4,8},{8,12},{12,16},{16,20},{20,24},{24,28},{28,0},{1,5},{5... | collective-permute-start | bytes 2359304 | tf_op jit(solution)/shard_map/ppermute | solution.py:164
  95.0 0.9 copy-start.5
  95.9 37.2 %collective-permute-start.3 = (bf16[1,4,2,16,3072]{4,3,2,1,0:T(8,128)(2,1)S(1)}, bf16[1,4,2,16,3072]{4,3,2,1,0:T(8,128)(2,1)S(1)}, u32[]{:S(2)}, u32[]{:S(2)}) collective-permute-start(bf16[1,4,2,16,3072]{4,3,2,1,0:T(8,128)(2,1)S(1)} %collective-permute-done.2), channel_id=1, source_target_pairs={{0,4},{4,8},{8,12},{12,16},{16,20},{20,24},{24,28},{28,0},{1,5},{5... | collective-permute-start | bytes 2359304 | tf_op jit(solution)/shard_map/ppermute | solution.py:164
  133.1 0.9 copy-start.7
  134.0 17.5 %collective-permute-start.4 = (bf16[1,4,2,16,3072]{4,3,2,1,0:T(8,128)(2,1)S(1)}, bf16[1,4,2,16,3072]{4,3,2,1,0:T(8,128)(2,1)}, u32[]{:S(2)}, u32[]{:S(2)}) collective-permute-start(bf16[1,4,2,16,3072]{4,3,2,1,0:T(8,128)(2,1)S(1)} %collective-permute-done.3), channel_id=1, source_target_pairs={{0,4},{4,8},{8,12},{12,16},{16,20},{20,24},{24,28},{28,0},{1,5},{5... | collective-permute-start | bytes 2359304 | tf_op jit(solution)/shard_map/ppermute | solution.py:164
  151.5 18.7 %collective-permute-start.5 = (bf16[1,4,2,16,3072]{4,3,2,1,0:T(8,128)(2,1)}, bf16[1,4,2,16,3072]{4,3,2,1,0:T(8,128)(2,1)}, u32[]{:S(2)}, u32[]{:S(2)}) collective-permute-start(bf16[1,4,2,16,3072]{4,3,2,1,0:T(8,128)(2,1)} %collective-permute-done.4), channel_id=1, source_target_pairs={{0,4},{4,8},{8,12},{12,16},{16,20},{20,24},{24,28},{28,0},{1,5},{5... | collective-permute-start | bytes 2359304 | tf_op jit(solution)/shard_map/ppermute | solution.py:164
  170.2 25.7 %collective-permute-start.6 = (bf16[1,4,2,16,3072]{4,3,2,1,0:T(8,128)(2,1)}, bf16[1,4,2,16,3072]{4,3,2,1,0:T(8,128)(2,1)}, u32[]{:S(2)}, u32[]{:S(2)}) collective-permute-start(bf16[1,4,2,16,3072]{4,3,2,1,0:T(8,128)(2,1)} %collective-permute-done.5), channel_id=1, source_target_pairs={{0,4},{4,8},{8,12},{12,16},{16,20},{20,24},{24,28},{28,0},{1,5},{5... | collective-permute-start | bytes 2359304 | tf_op jit(solution)/shard_map/ppermute | solution.py:164
  171.3 288.2 %all-reduce.3.cloned.1.call-start = ((), (), s32[]{:S(2)}) async-start(), calls=%async_computation.4 | async-start | bytes 12582912
  194.5 5.2 %copy-start.8 = (bf16[1,4,2,16,3072]{4,3,2,1,0:T(8,128)(2,1)S(1)}, bf16[1,4,2,16,3072]{4,3,2,1,0:T(8,128)(2,1)}, u32[]{:S(2)}) copy-start(bf16[1,4,2,16,3072]{4,3,2,1,0:T(8,128)(2,1)} %copy-done.7) | copy-start | bytes 2359300
  194.5 5.3 %copy-start.6 = (bf16[1,4,2,16,3072]{4,3,2,1,0:T(8,128)(2,1)S(1)}, bf16[1,4,2,16,3072]{4,3,2,1,0:T(8,128)(2,1)}, u32[]{:S(2)}) copy-start(bf16[1,4,2,16,3072]{4,3,2,1,0:T(8,128)(2,1)} %copy-done.5) | copy-start | bytes 2359300
  194.5 5.3 %copy-start.4 = (bf16[1,4,2,16,3072]{4,3,2,1,0:T(8,128)(2,1)S(1)}, bf16[1,4,2,16,3072]{4,3,2,1,0:T(8,128)(2,1)}, u32[]{:S(2)}) copy-start(bf16[1,4,2,16,3072]{4,3,2,1,0:T(8,128)(2,1)} %copy-done.3) | copy-start | bytes 2359300
  194.5 5.4 %copy-start.2 = (bf16[1,4,2,16,3072]{4,3,2,1,0:T(8,128)(2,1)S(1)}, bf16[1,4,2,16,3072]{4,3,2,1,0:T(8,128)(2,1)}, u32[]{:S(2)}) copy-start(bf16[1,4,2,16,3072]{4,3,2,1,0:T(8,128)(2,1)} %copy-done.1) | copy-start | bytes 2359300
  272.6 196.1 %copy-start.9 = (bf16[128,8,128]{0,2,1:T(8,128)(2,1)S(1)}, bf16[128,8,128]{0,2,1:T(8,128)(2,1)}, u32[]{:S(2)}) copy-start(bf16[128,8,128]{0,2,1:T(8,128)(2,1)} %fusion.54) | copy-start | bytes 786436
  462.3 15.1 %all-to-all-start.1 = ((bf16[4,2,16,3072]{3,2,1,0:T(8,128)(2,1)}), bf16[4,2,16,3072]{3,2,1,0:T(8,128)(2,1)S(1)}, u32[]{:S(2)}, u32[]{:S(2)}) async-start(bf16[4,2,16,3072]{3,2,1,0:T(8,128)(2,1)} %copy.168), calls=%async_computation.1 | async-start | bytes 1572864 | tf_op jit(solution)/shard_map/all_to_all | solution.py:174
Sparse Core Ops, SparseCore 0:
  52.9 77.3 all-gather.7
  171.4 49.8 all-gather.5
  251.2 208.2 all-reduce.2
